TPU v7x, 32 devices: a whole 2x2x4 slice. The times are simulated.
32 devices in a mesh: track: 4 (over y, x), tm: 8 (over z, core).
Axes of the slice: x: 2, y: 2, z: 4, core: 2. Of those that a mesh axis runs over, the one named last changes fastest.
Arguments:
- observations: float32 [1024, 16, 128], P('tm', 'track'), may hold values from -18 to 18
- dynamics: bfloat16 [256, 128, 128], P('track'), may hold values from -1 to 1
- smoother_gain: bfloat16 [256, 128, 128], P('track'), may hold values from -1 to 1
- gains: bfloat16 [256, 128], P('track'), may hold values from 0 to 1
- regime: int32 [256], P('tm'), may hold values from 0 to 255
Outputs:
- smoothed: float32 [1024, 16, 128], P('tm', 'track')
All inputs are finite; a program needn't handle non-finite values.
Results may differ from a plain program's by a relative error of at most 0.0003.
Values may be sent and summed in bfloat16 or wider, within the bound.
No kernel may reach another device: no remote copies, remote signals or barrier semaphores. Data moves between devices by JAX's collectives and lax.ppermute only.
A program may use at most 64 MiB of HBM per device.

v0:
```python
import jax
import jax.numpy as jnp
import numpy as np
from jax import lax
from jax.sharding import PartitionSpec as P


def prefix(shard, axis, combine, identity, reverse):
    peers, position = (lax.axis_size(axis), lax.axis_index(axis))
    everything = jax.tree.map(lambda part: lax.all_gather(part, axis), shard)
    start = jax.tree.map(
        lambda part, zero: jnp.broadcast_to(jnp.asarray(zero, part.dtype), part.shape),
        shard,
        identity,
    )

    def step(k, before):
        at = peers - 1 - k if reverse else k
        reached = at > position if reverse else at < position
        new = combine(before, jax.tree.map(lambda part: part[at], everything))
        return jax.tree.map(lambda a, b: jnp.where(reached, a, b), new, before)

    return lax.fori_loop(0, peers, step, start)


def from_root(shard, axis, root):
    mine = lax.axis_index(axis) == root
    return lax.psum(jnp.where(mine, shard, jnp.zeros_like(shard)), axis)


def shifted(value, axis, steps):
    count = lax.axis_size(axis)
    initial, last = (max(0, -steps), min(count, count - steps))
    return lax.ppermute(value, axis, [(source, source + steps) for source in range(initial, last)])


def matmul(left, right):
    return jnp.dot(left, right, precision=lax.Precision.HIGHEST)


def compose(earlier, later):
    return (matmul(earlier[0], later[0]), matmul(earlier[1], later[0]) + later[1])


def carried_forward(pair):
    width = pair[0].shape[0]
    identity_pair = (jnp.eye(width, dtype=jnp.float32), jnp.zeros_like(pair[1]))
    return prefix(pair, "tm", compose, identity_pair, False)[1]


def carried_backward(pair):
    width = pair[0].shape[0]
    identity_pair = (jnp.eye(width, dtype=jnp.float32), jnp.zeros_like(pair[1]))
    return prefix(pair, "tm", compose, identity_pair, True)[1]


def spread_forward(pair):
    width = pair[0].shape[0]
    identity_pair = (jnp.eye(width, dtype=jnp.float32), jnp.zeros_like(pair[1]))
    within = prefix(pair, "track", compose, identity_pair, False)
    through = compose(within, pair)
    joined = jnp.concatenate([through[0], through[1]], axis=0)
    total = from_root(joined, "track", lax.axis_size("track") - 1)
    earlier = carried_forward((total[:width], total[width:]))
    return matmul(earlier, within[0]) + within[1]


def spread_backward(pair):
    width = pair[0].shape[0]
    identity_pair = (jnp.eye(width, dtype=jnp.float32), jnp.zeros_like(pair[1]))
    within = prefix(pair, "track", compose, identity_pair, True)
    through = compose(within, pair)
    joined = jnp.concatenate([through[0], through[1]], axis=0)
    total = from_root(joined, "track", 0)
    later = carried_backward((total[:width], total[width:]))
    return matmul(later, within[0]) + within[1]


def pick_rows(block_ids, dynamics, smoother_gain, gains):
    owned = dynamics.shape[0]
    width = dynamics.shape[1]
    offset = lax.axis_index("track") * owned
    selector = (block_ids[:, None] - offset == jnp.arange(owned, dtype=jnp.int32)[None, :]).astype(
        jnp.bfloat16
    )
    pick_dyn = jnp.dot(
        selector, dynamics.reshape(owned, width * width), preferred_element_type=jnp.float32
    )
    pick_smooth = jnp.dot(
        selector, smoother_gain.reshape(owned, width * width), preferred_element_type=jnp.float32
    )
    pick_gain = jnp.dot(selector, gains, preferred_element_type=jnp.float32)
    return (pick_dyn, pick_smooth, pick_gain)


def local_map(carry, inputs):
    matrix, vector = inputs
    return ((matmul(carry[0], matrix), matmul(carry[1], matrix) + vector), None)


def propagate(state, inputs):
    matrix, vector = inputs
    state = matmul(state, matrix) + vector
    return (state, state)


def retreat(state, inputs):
    matrix, vector = inputs
    state = vector + matmul(state, matrix)
    return (state, state)


def smooth_span(picked, measured, dwell, finishing, forward_carry, backward_carry):
    pick_dyn, pick_smooth, pick_gain = picked
    length, tracks, width = measured.shape
    count = pick_gain.shape[0]
    step_dyn = jnp.repeat(pick_dyn.reshape(count, width, width), dwell, axis=0)
    step_smooth = jnp.repeat(pick_smooth.reshape(count, width, width), dwell, axis=0)
    step_gain = jnp.repeat(pick_gain, dwell, axis=0)[:length]
    current = step_dyn[:length]
    upcoming = step_dyn[1 : length + 1]
    final_row = jnp.arange(length) == length - 1
    live = jnp.where(jnp.logical_and(finishing, final_row), 0.0, 1.0).astype(jnp.float32)
    next_gain = step_smooth[1 : length + 1] * live[:, None, None]
    closed = jnp.swapaxes(current, 1, 2) * (1.0 - step_gain)[:, None, :]
    driven = step_gain[:, None, :] * measured
    empty_vec = jnp.zeros((tracks, width), jnp.float32)
    unit_mat = jnp.eye(width, dtype=jnp.float32)
    filter_pair, _ = lax.scan(local_map, (unit_mat, empty_vec), (closed, driven))
    before = forward_carry(filter_pair)
    _, filtered = lax.scan(propagate, before, (closed, driven))
    cross = jnp.einsum("tij,tjk->tik", next_gain, upcoming, precision=lax.Precision.HIGHEST)
    innovation = filtered - jnp.einsum(
        "tbj,tij->tbi", filtered, cross, precision=lax.Precision.HIGHEST
    )
    gain_rows = jnp.swapaxes(next_gain, 1, 2)
    smooth_pair, _ = lax.scan(
        local_map, (unit_mat, empty_vec), (gain_rows, innovation), reverse=True
    )
    after = backward_carry(smooth_pair)
    _, smoothed = lax.scan(retreat, after, (gain_rows, innovation), reverse=True)
    return smoothed


def body(observations, dynamics, smoother_gain, gains, regime):
    length = observations.shape[0]
    blocks = regime.shape[0]
    dwell = length // blocks
    following = shifted(regime[:1], "tm", -1)
    block_ids = jnp.concatenate([regime, following])
    on_last = lax.axis_index("tm") == lax.axis_size("tm") - 1
    groups = lax.axis_size("track")
    share = blocks // groups
    place = lax.axis_index("track")
    order = (np.arange(groups)[:, None] * share + np.arange(share + 1)[None, :]).reshape(-1)
    spread_ids = block_ids[order]
    picked = pick_rows(spread_ids, dynamics, smoother_gain, gains)
    picked = (
        lax.psum_scatter(
            picked[0].astype(jnp.bfloat16), "track", scatter_dimension=0, tiled=True
        ).astype(jnp.float32),
        lax.psum_scatter(
            picked[1].astype(jnp.bfloat16), "track", scatter_dimension=0, tiled=True
        ).astype(jnp.float32),
        lax.psum_scatter(
            picked[2].astype(jnp.bfloat16), "track", scatter_dimension=0, tiled=True
        ).astype(jnp.float32),
    )
    measured = lax.all_to_all(observations, "track", split_axis=0, concat_axis=1, tiled=True)
    finishing = jnp.logical_and(on_last, place == groups - 1)
    smoothed = smooth_span(picked, measured, dwell, finishing, spread_forward, spread_backward)
    return lax.all_to_all(smoothed, "track", split_axis=1, concat_axis=0, tiled=True)


def solution(mesh):
    placed = (
        P("tm", "track", None),
        P("track", None, None),
        P("track", None, None),
        P("track", None),
        P("tm"),
    )
    return jax.shard_map(
        body, mesh=mesh, in_specs=placed, out_specs=P("tm", "track", None), check_vma=False
    )
```

profile of v0, /device:TPU:0, one launch (start us, length us, event | category | flops | bytes accessed | tf_op | source)
XLA Modules:
  0.0 525.0 jit_solution(3427825557945967753)
XLA Ops:
  6.5 1.4 collective-permute-start
  8.6 1.2 collective-permute-done
  9.8 1.4 pad_add_fusion
  12.0 4.2 convolution_convert_fusion
  16.2 2.6 convolution_convert_fusion.1
  18.9 5.2 all-to-all-start
  25.6 17.5 %all-reduce.2 = bf16[36,128]{1,0:T(8,128)(2,1)S(1)} all-reduce(bf16[36,128]{1,0:T(8,128)(2,1)S(1)} %convolution_convert_fusion.2), channel_id=12, replica_groups=mesh['track'=4,'tm'=8] {'track'}, use_global_device_ids=true, to_apply=%region_2.0.clone | all-reduce | flops 4608 | bytes 18432
  43.2 58.4 %all-reduce.12.cloned.1.call-done = (bf16[36,16384]{1,0:T(8,128)(2,1)}, bf16[36,16384]{1,0:T(8,128)(2,1)}) async-done(((bf16[36,16384]{1,0:T(8,128)(2,1)}, bf16[36,16384]{1,0:T(8,128)(2,1)}), (bf16[36,16384]{1,0:T(8,128)(2,1)}, bf16[36,16384]{1,0:T(8,128)(2,1)})) %all-reduce.12.cloned.1.call-update) | async-done | bytes 2359312
  101.5 1.6 dynamic-slice_convert_fusion
  104.0 1.3 copy.21
  105.3 1.5 bitcast_multiply_fusion
  106.8 70.1 %while.124 = (s32[]{:T(128)}, f32[128,128]{0,1:T(8,128)S(1)}, f32[16,128]{1,0:T(8,128)S(1)}, f32[32,128,128]{2,1,0:T(8,128)}, f32[32,16,128]{2,1,0:T(8,128)S(1)}, /*index=5*/s32[]{:T(128)}, s32[]{:T(128)}) while((s32[]{:T(128)}, f32[128,128]{0,1:T(8,128)S(1)}, f32[16,128]{1,0:T(8,128)S(1)}, f32[32,128,128]{2,1,0:T(8,128)}, ...), condition=%wide.region_4.5_spmd.clone, body=%wide.region_3.4_spmd.clone.sunk | while | flops 28315648 | bytes 435799 | solution.py:129
  177.0 10.0 %all-gather = f32[512,128]{0,1:T(8,128)S(1)} all-gather(f32[128,128]{0,1:T(8,128)S(1)} %get-tuple-element.758), channel_id=2, replica_groups=mesh['track'=4,'tm'=8] {'track'}, dimensions={0}, use_global_device_ids=true | all-gather | bytes 327680 | tf_op jit(solution)/shard_map/all_gather | solution.py:10
  187.1 7.2 %all-gather.1 = f32[64,128]{1,0:T(8,128)S(1)} all-gather(f32[16,128]{1,0:T(8,128)S(1)} %get-tuple-element.759), channel_id=3, replica_groups=mesh['track'=4,'tm'=8] {'track'}, dimensions={0}, use_global_device_ids=true | all-gather | bytes 40960 | tf_op jit(solution)/shard_map/all_gather | solution.py:10
  194.3 2.1 while.125
  199.0 3.6 fusion.78
  202.6 1.5 fusion.80
  204.1 34.3 %all-reduce.8.cloned.1.call-done = f32[144,128]{1,0:T(8,128)} async-done(((f32[144,128]{1,0:T(8,128)}), f32[144,128]{1,0:T(8,128)}) %all-reduce.8.cloned.1.call-update) | async-done | bytes 73744 | tf_op jit(solution)/shard_map/psum | solution.py:28
  239.3 14.7 %all-gather.2 = f32[1024,128]{1,0:T(8,128)S(1)} all-gather(f32[128,128]{1,0:T(8,128)S(1)} %slice.58), channel_id=4, replica_groups=mesh['track'=4,'tm'=8] {'tm'}, dimensions={0}, use_global_device_ids=true | all-gather | bytes 589824 | tf_op jit(solution)/shard_map/all_gather | solution.py:10
  254.7 14.3 %all-gather.3 = f32[128,128]{1,0:T(8,128)S(1)} all-gather(f32[16,128]{1,0:T(8,128)S(1)} %slice.59), channel_id=5, replica_groups=mesh['track'=4,'tm'=8] {'tm'}, dimensions={0}, use_global_device_ids=true | all-gather | bytes 73728 | tf_op jit(solution)/shard_map/all_gather | solution.py:10
  269.0 1.5 while.126
  270.7 32.9 %while.122 = (s32[]{:T(128)}, f32[16,128]{1,0:T(8,128)S(1)}, f32[32,16,128]{2,1,0:T(8,128)S(1)}, f32[32,128,128]{2,1,0:T(8,128)}, f32[32,16,128]{2,1,0:T(8,128)}, /*index=5*/s32[]{:T(128)}) while((s32[]{:T(128)}, f32[16,128]{1,0:T(8,128)S(1)}, f32[32,16,128]{2,1,0:T(8,128)S(1)}, f32[32,128,128]{2,1,0:T(8,128)}, f32[32,16,128]{2,1,0:T(8,128)}, ...), condition=%wide.region_11.12_spmd, body=%wide.region_10.11_spmd.sunk | while | flops 3147778 | bytes 115781 | solution.py:131
  303.6 3.4 convolution_subtract_fusion
  307.0 70.2 %while.127 = (s32[]{:T(128)}, f32[128,128]{0,1:T(8,128)S(1)}, f32[16,128]{1,0:T(8,128)S(1)}, f32[32,128,128]{2,1,0:T(8,128)}, f32[32,16,128]{2,1,0:T(8,128)S(1)}, /*index=5*/s32[]{:T(128)}, s32[]{:T(128)}, s32[]{:T(128)}) while((s32[]{:T(128)}, f32[128,128]{0,1:T(8,128)S(1)}, f32[16,128]{1,0:T(8,128)S(1)}, ...), condition=%wide.region_13.14_spmd.clone, body=%wide.region_12.13_spmd.clone.sunk | while | flops 28315652 | bytes 435822 | solution.py:137
  308.1 1.1 convolution_bitcast_fusion.15
  310.2 1.1 convolution_bitcast_fusion.15
  312.4 1.1 convolution_bitcast_fusion.15
  314.6 1.1 convolution_bitcast_fusion.15
  316.8 1.1 convolution_bitcast_fusion.15
  319.0 1.1 convolution_bitcast_fusion.15
  321.2 1.1 convolution_bitcast_fusion.15
  323.4 1.1 convolution_bitcast_fusion.15
  325.6 1.1 convolution_bitcast_fusion.15
  327.8 1.1 convolution_bitcast_fusion.15
  330.0 1.1 convolution_bitcast_fusion.15
  332.2 1.1 convolution_bitcast_fusion.15
  334.4 1.1 convolution_bitcast_fusion.15
  336.6 1.1 convolution_bitcast_fusion.15
  338.8 1.1 convolution_bitcast_fusion.15
  341.0 1.1 convolution_bitcast_fusion.15
  343.1 1.1 convolution_bitcast_fusion.15
  345.3 1.1 convolution_bitcast_fusion.15
  347.5 1.1 convolution_bitcast_fusion.15
  349.7 1.1 convolution_bitcast_fusion.15
  351.9 1.1 convolution_bitcast_fusion.15
  354.1 1.1 convolution_bitcast_fusion.15
  356.3 1.1 convolution_bitcast_fusion.15
  358.5 1.1 convolution_bitcast_fusion.15
  360.7 1.1 convolution_bitcast_fusion.15
  362.9 1.1 convolution_bitcast_fusion.15
  365.1 1.1 convolution_bitcast_fusion.15
  367.3 1.1 convolution_bitcast_fusion.15
  371.7 1.1 convolution_bitcast_fusion.15
  373.8 1.1 convolution_bitcast_fusion.15
  376.0 1.1 convolution_bitcast_fusion.15
  377.2 10.7 %all-gather.4 = f32[512,128]{0,1:T(8,128)S(1)} all-gather(f32[128,128]{0,1:T(8,128)S(1)} %get-tuple-element.764), channel_id=6, replica_groups=mesh['track'=4,'tm'=8] {'track'}, dimensions={0}, use_global_device_ids=true | all-gather | bytes 327680 | tf_op jit(solution)/shard_map/all_gather | solution.py:10
  388.1 8.1 %all-gather.5 = f32[64,128]{1,0:T(8,128)S(1)} all-gather(f32[16,128]{1,0:T(8,128)S(1)} %get-tuple-element.765), channel_id=7, replica_groups=mesh['track'=4,'tm'=8] {'track'}, dimensions={0}, use_global_device_ids=true | all-gather | bytes 40960 | tf_op jit(solution)/shard_map/all_gather | solution.py:10
  396.2 2.1 while.128
  399.5 40.9 %all-reduce.10.cloned.1.call-done = f32[144,128]{1,0:T(8,128)} async-done(((f32[144,128]{1,0:T(8,128)}), f32[144,128]{1,0:T(8,128)}) %all-reduce.10.cloned.1.call-update) | async-done | bytes 73744 | tf_op jit(solution)/shard_map/psum | solution.py:28
  441.3 14.7 %all-gather.6 = f32[1024,128]{1,0:T(8,128)S(1)} all-gather(f32[128,128]{1,0:T(8,128)S(1)} %slice.61), channel_id=8, replica_groups=mesh['track'=4,'tm'=8] {'tm'}, dimensions={0}, use_global_device_ids=true | all-gather | bytes 589824 | tf_op jit(solution)/shard_map/all_gather | solution.py:10
  456.7 14.0 %all-gather.7 = f32[128,128]{1,0:T(8,128)S(1)} all-gather(f32[16,128]{1,0:T(8,128)S(1)} %slice.62), channel_id=9, replica_groups=mesh['track'=4,'tm'=8] {'tm'}, dimensions={0}, use_global_device_ids=true | all-gather | bytes 73728 | tf_op jit(solution)/shard_map/all_gather | solution.py:10
  470.7 1.5 while.129
  472.4 35.0 %while.123 = (s32[]{:T(128)}, f32[16,128]{1,0:T(8,128)S(1)}, f32[32,16,128]{2,0,1:T(8,128)S(1)}, f32[32,16,128]{2,1,0:T(8,128)S(1)}, f32[32,128,128]{2,1,0:T(8,128)}, /*index=5*/s32[]{:T(128)}, s32[]{:T(128)}, s32[]{:T(128)}) while((s32[]{:T(128)}, f32[16,128]{1,0:T(8,128)S(1)}, f32[32,16,128]{2,0,1:T(8,128)S(1)}, ...), condition=%wide.region_20.21_spmd, body=%wide.region_19.20_spmd.sunk | while | flops 3147779 | bytes 124005 | solution.py:141
  507.4 10.1 %all_to_all.36 = f32[32,16,128]{2,0,1:T(8,128)S(1)} all-to-all(f32[32,16,128]{2,0,1:T(8,128)S(1)} %get-tuple-element.769), channel_id=1, replica_groups=mesh['track'=4,'tm'=8] {'track'}, dimensions={1} | all-to-all | bytes 524288 | tf_op jit(solution)/shard_map/all_to_all | solution.py:172
  (519 shorter events, 187.5 us)
Async XLA Ops:
  6.5 18.8 %copy-start = (bf16[64,128]{1,0:T(8,128)(2,1)S(1)}, bf16[64,128]{1,0:T(8,128)(2,1)}, u32[]{:S(2)}) copy-start(bf16[64,128]{1,0:T(8,128)(2,1)} %param.26) | copy-start | bytes 49156
  6.5 9.7 %copy-start.6 = (bf16[64,128,128]{2,1,0:T(8,128)(2,1)S(1)}, bf16[64,128,128]{2,1,0:T(8,128)(2,1)}, u32[]{:S(2)}) copy-start(bf16[64,128,128]{2,1,0:T(8,128)(2,1)} %param.25) | copy-start | bytes 6291460
  6.5 95.0 %all-reduce.12.cloned.1.call-start = ((), (), s32[]{:S(2)}) async-start(), calls=%async_computation.4 | async-start | bytes 5242880
  6.5 3.3 collective-permute-start
  18.9 5.3 %copy-start.9 = (u32[32]{0:T(128)S(1)}, u32[32]{0:T(128)}, u32[]{:S(2)}) copy-start(u32[32]{0:T(128)} %constant.255) | copy-start | bytes 388
  18.9 24.2 %all-to-all-start = ((f32[128,4,128]{2,1,0:T(4,128)}), f32[128,4,128]{2,1,0:T(4,128)S(1)}, u32[]{:S(2)}, u32[]{:S(2)}) async-start(f32[128,4,128]{2,1,0:T(4,128)} %param.23), calls=%async_computation | async-start | bytes 524288 | tf_op jit(solution)/shard_map/all_to_all | solution.py:169
  24.1 214.4 %all-reduce.8.cloned.1.call-start = ((), (), s32[]{:S(2)}) async-start(), calls=%async_computation.2 | async-start | bytes 147456 | tf_op jit(solution)/shard_map/psum | solution.py:28
  24.1 79.0 %copy-start.1 = (f32[128,128]{0,1:T(8,128)}, f32[128,128]{0,1:T(8,128)S(1)}, u32[]{:S(2)}) copy-start(f32[128,128]{0,1:T(8,128)S(1)} %fusion.82) | copy-start | bytes 196612
  104.0 2.8 copy-start.3
  106.8 87.5 %copy-start.4 = (f32[128,128]{0,1:T(8,128)S(1)}, f32[128,128]{0,1:T(8,128)}, u32[]{:S(2)}) copy-start(f32[128,128]{0,1:T(8,128)} %copy-done.1) | copy-start | bytes 196612
  176.9 20.7 %copy-start.7 = (f32[32,16,128]{2,1,0:T(8,128)}, f32[32,16,128]{2,1,0:T(8,128)S(1)}, u32[]{:S(2)}) copy-start(f32[32,16,128]{2,1,0:T(8,128)S(1)} %get-tuple-element.1440) | copy-start | bytes 786436
  197.6 242.8 %all-reduce.10.cloned.1.call-start = ((), (), s32[]{:S(2)}) async-start(), calls=%async_computation.3 | async-start | bytes 147456 | tf_op jit(solution)/shard_map/psum | solution.py:28
  202.6 68.1 %copy-start.8 = (f32[32,16,128]{2,1,0:T(8,128)S(1)}, f32[32,16,128]{2,1,0:T(8,128)}, u32[]{:S(2)}) copy-start(f32[32,16,128]{2,1,0:T(8,128)} %custom-call.8) | copy-start | bytes 786436
  254.7 52.2 %copy-start.5 = (f32[128,128]{0,1:T(8,128)S(1)}, f32[128,128]{0,1:T(8,128)}, u32[]{:S(2)}) copy-start(f32[128,128]{0,1:T(8,128)} %copy-done.1) | copy-start | bytes 196612
  307.0 89.2 %copy-start.2 = (f32[128,128]{0,1:T(8,128)S(1)}, f32[128,128]{0,1:T(8,128)}, u32[]{:S(2)}) copy-start(f32[128,128]{0,1:T(8,128)} %copy-done.1) | copy-start | bytes 196612
Sparse Core Ops, SparseCore 0:
  19.0 82.4 all-reduce.11
  197.7 40.6 all-reduce.7
  399.6 40.7 all-reduce.9
where the time goes:
time: 535 us; the launch traced here: 525 us
  matrix products  223 us (42%)
  waiting for transfers between devices  135 us (25%)
  blocking collectives  121 us (23%)
  between operations  14.1 us (3%)
  local copies, waits for them, and re-layouts  12.8 us (2%)
  other arithmetic  8.16 us (2%)
  starting transfers between devices  6.66 us (1%)
    dot_general x230, matrix products, matmul(): return jnp.dot(left, right, precision=lax.Precision.HIGHEST)  208 us
    all_gather x8, blocking collectives, prefix(): everything = jax.tree.map(lambda part: lax.all_gather(part, axis), shard)  93.8 us
    psum x2, waiting for transfers between devices, from_root(): return lax.psum(jnp.where(mine, shard, jnp.zeros_like(shard)), axis)  75.2 us
    unnamed x4, waiting for transfers between devices  58.4 us
    unnamed x1, blocking collectives  17.5 us
  transfers between devices with their start and end apart: 5, of which 4 were waited for; matrix products, arithmetic and copies ran while one was open for 2% of the time, Pallas kernels for 0%

commit v1 on v0

--- a/solution.py
+++ b/solution.py
@@ -25,7 +25,7 @@
 
 def from_root(shard, axis, root):
     mine = lax.axis_index(axis) == root
-    return lax.psum(jnp.where(mine, shard, jnp.zeros_like(shard)), axis)
+    return jnp.sum(lax.all_gather(jnp.where(mine, shard, jnp.zeros_like(shard)), axis), axis=0)
 
 
 def shifted(value, axis, steps):

time: 535 us -> 421 us (0.79)
  matrix products: 223 us -> 141 us
  waiting for transfers between devices: 135 us -> 58.4 us
  local copies, waits for them, and re-layouts: 12.8 us -> 41.9 us
  blocking collectives: 121 us -> 140 us
    dot_general x230, matrix products: 208 us -> 127 us  [matmul(): return jnp.dot(left, right, precision=lax.Precision.HIGHEST)]
    psum x2 -> x0, waiting for transfers between devices: 75.2 us -> none  [from_root(): return lax.psum(jnp.where(mine, shard, jnp.zeros_like(shard)), axis)]
    while x224, local copies, waits for them, and re-layouts: 1.96 us -> 31.8 us
    all_gather x0 -> x2, blocking collectives: none -> 17.8 us  [from_root(): lax.all_gather(jnp.where(mine, shard, jnp.zeros_like(shard)), axis)]
    unnamed x4 -> x2, waiting for transfers between devices: 58.4 us -> 57.2 us
  transfers between devices with their start and end apart: 5 -> 3, of which waited for: 4 -> 2; matrix products, arithmetic and copies ran while one was open for 2% -> 1% of each run, Pallas kernels for 0% -> 0%
where the time goes in v1:
time: 421 us; the launch traced here: 414 us
  matrix products  141 us (33%)
  blocking collectives  140 us (33%)
  waiting for transfers between devices  58.4 us (14%)
  local copies, waits for them, and re-layouts  41.9 us (10%)
  between operations  14.5 us (3%)
  other arithmetic  8.46 us (2%)
  starting transfers between devices  6.62 us (2%)
    dot_general x230, matrix products, matmul(): return jnp.dot(left, right, precision=lax.Precision.HIGHEST)  127 us
    all_gather x8, blocking collectives, prefix(): everything = jax.tree.map(lambda part: lax.all_gather(part, axis), shard)  95.5 us
    unnamed x2, waiting for transfers between devices  57.2 us
    while x224, local copies, waits for them, and re-layouts  31.8 us
    all_gather x2, blocking collectives, from_root(): lax.all_gather(jnp.where(mine, shard, jnp.zeros_like(shard)), axis)  17.8 us
    unnamed x1, blocking collectives  17.5 us
    all_to_all x1, blocking collectives, body(): lax.all_to_all(smoothed, 'track', split_axis=1, concat_axis=0, tiled=True)  8.89 us
  transfers between devices with their start and end apart: 3, of which 2 were waited for; matrix products, arithmetic and copies ran while one was open for 1% of the time, Pallas kernels for 0%

profile of v1, /device:TPU:0, one launch (start us, length us, event | category | flops | bytes accessed | tf_op | source)
XLA Modules:
  0.0 413.9 jit_solution(17440477247368876040)
XLA Ops:
  12.0 4.2 %convolution_convert_fusion = bf16[36,16384]{1,0:T(8,128)(2,1)} fusion(bf16[8,8,128,128]{3,2,1,0:T(8,128)(2,1)} %bitcast.264, s32[36]{0:T(128)S(1)} %broadcast_subtract_fusion.1), kind=kOutput, calls=%fused_computation.88 | convolution fusion | flops 76089600 | bytes 3276944 | tf_op jit(solution)/shard_map/dot_general | solution.py:86
  16.2 2.6 convolution_convert_fusion.1
  18.9 5.2 %all-to-all-start = ((f32[128,4,128]{2,1,0:T(4,128)}), f32[128,4,128]{2,1,0:T(4,128)S(1)}, u32[]{:S(2)}, u32[]{:S(2)}) async-start(f32[128,4,128]{2,1,0:T(4,128)} %param.23), calls=%async_computation | async-start | bytes 524288 | tf_op jit(solution)/shard_map/all_to_all | solution.py:169
  26.2 17.5 %all-reduce.2 = bf16[36,128]{1,0:T(8,128)(2,1)S(1)} all-reduce(bf16[36,128]{1,0:T(8,128)(2,1)S(1)} %convolution_convert_fusion.2), channel_id=12, replica_groups=mesh['track'=4,'tm'=8] {'track'}, use_global_device_ids=true, to_apply=%region_2.0.clone | all-reduce | flops 4608 | bytes 18432
  44.4 57.2 %all-reduce.6.cloned.1.call-done = (bf16[36,16384]{1,0:T(8,128)(2,1)}, bf16[36,16384]{1,0:T(8,128)(2,1)}) async-done(((bf16[36,16384]{1,0:T(8,128)(2,1)}, bf16[36,16384]{1,0:T(8,128)(2,1)}), (bf16[36,16384]{1,0:T(8,128)(2,1)}, bf16[36,16384]{1,0:T(8,128)(2,1)})) %all-reduce.6.cloned.1.call-update) | async-done | bytes 2359312
  101.5 2.6 dynamic-slice_convert_fusion
  106.5 57.3 %while.124 = (s32[]{:T(128)}, f32[128,128]{0,1:T(8,128)S(1)}, f32[16,128]{1,0:T(8,128)}, f32[32,128,128]{2,1,0:T(8,128)S(1)}, f32[32,16,128]{2,1,0:T(8,128)S(1)}, /*index=5*/s32[]{:T(128)}, s32[]{:T(128)}) while((s32[]{:T(128)}, f32[128,128]{0,1:T(8,128)S(1)}, f32[16,128]{1,0:T(8,128)}, f32[32,128,128]{2,1,0:T(8,128)S(1)}, ...), condition=%wide.region_4.5_spmd.clone, body=%wide.region_3.4_spmd.clone.sunk | while | flops 28315648 | bytes 435291 | solution.py:129
  164.5 10.6 %all-gather = f32[512,128]{0,1:T(8,128)} all-gather(f32[128,128]{0,1:T(8,128)S(1)} %get-tuple-element.758), channel_id=2, replica_groups=mesh['track'=4,'tm'=8] {'track'}, dimensions={0}, use_global_device_ids=true | all-gather | bytes 327680 | tf_op jit(solution)/shard_map/all_gather | solution.py:10
  176.2 8.6 %all-gather.1 = f32[64,128]{1,0:T(8,128)} all-gather(f32[16,128]{1,0:T(8,128)} %get-tuple-element.759), channel_id=3, replica_groups=mesh['track'=4,'tm'=8] {'track'}, dimensions={0}, use_global_device_ids=true | all-gather | bytes 40960 | tf_op jit(solution)/shard_map/all_gather | solution.py:10
  184.8 9.9 %while.125 = (s32[]{:T(128)}, f32[128,128]{0,1:T(8,128)S(1)}, f32[16,128]{1,0:T(8,128)}, s32[]{:T(128)}, f32[4,128,128]{2,1,0:T(8,128)S(1)}, /*index=5*/f32[4,16,128]{2,1,0:T(8,128)}, s32[]{:T(128)}, s32[]{:T(128)}) while((s32[]{:T(128)}, f32[128,128]{0,1:T(8,128)S(1)}, f32[16,128]{1,0:T(8,128)}, s32[]{:T(128)}, ...), condition=%wide.region_6.7_spmd.clone, body=%wide.region_5.6_spmd.clone.sunk | while | flops 28336132 | bytes 510572 | solution.py:23
  196.0 9.0 %all_gather.60 = f32[4,144,128]{2,1,0:T(8,128)} all-gather(f32[1,144,128]{2,1,0:T(8,128)S(1)} %maximum_select_fusion), channel_id=1, replica_groups=mesh['track'=4,'tm'=8] {'track'}, dimensions={0}, use_global_device_ids=true | all-gather | bytes 368640 | tf_op jit(solution)/shard_map/all_gather | solution.py:28
  206.0 15.8 %all-gather.2 = f32[1024,128]{1,0:T(8,128)} all-gather(f32[128,128]{1,0:T(8,128)S(1)} %slice.58), channel_id=4, replica_groups=mesh['track'=4,'tm'=8] {'tm'}, dimensions={0}, use_global_device_ids=true | all-gather | bytes 589824 | tf_op jit(solution)/shard_map/all_gather | solution.py:10
  221.8 14.2 %all-gather.3 = f32[128,128]{1,0:T(8,128)S(1)} all-gather(f32[16,128]{1,0:T(8,128)S(1)} %slice.59), channel_id=5, replica_groups=mesh['track'=4,'tm'=8] {'tm'}, dimensions={0}, use_global_device_ids=true | all-gather | bytes 73728 | tf_op jit(solution)/shard_map/all_gather | solution.py:10
  235.9 18.5 %while.126 = (s32[]{:T(128)}, f32[16,128]{1,0:T(8,128)}, s32[]{:T(128)}, f32[8,128,128]{2,1,0:T(8,128)}, f32[8,16,128]{2,1,0:T(8,128)S(1)}, /*index=5*/s32[]{:T(128)}, s32[]{:T(128)}) while((s32[]{:T(128)}, f32[16,128]{1,0:T(8,128)}, s32[]{:T(128)}, f32[8,128,128]{2,1,0:T(8,128)}, f32[8,16,128]{2,1,0:T(8,128)S(1)}, ...), condition=%wide.region_9.10_spmd.clone, body=%wide.region_8.9_spmd.clone.sunk | while | flops 3153924 | bytes 117343 | solution.py:23
  236.6 1.6 fusion.158
  238.9 1.6 fusion.158
  241.2 1.6 fusion.158
  243.5 1.6 fusion.158
  245.8 1.6 fusion.158
  248.2 1.6 fusion.158
  250.5 1.6 fusion.158
  252.8 1.6 fusion.158
  255.2 47.1 %while.122 = (s32[]{:T(128)}, f32[16,128]{1,0:T(8,128)S(1)}, f32[32,16,128]{2,1,0:T(8,128)}, f32[32,128,128]{2,1,0:T(8,128)S(1)}, f32[32,16,128]{2,1,0:T(8,128)}, /*index=5*/s32[]{:T(128)}) while((s32[]{:T(128)}, f32[16,128]{1,0:T(8,128)S(1)}, f32[32,16,128]{2,1,0:T(8,128)}, f32[32,128,128]{2,1,0:T(8,128)S(1)}, f32[32,16,128]{2,1,0:T(8,128)}, ...), condition=%wide.region_11.12_spmd, body=%wide.region_10.11_spmd.sunk | while | flops 3147778 | bytes 115781 | solution.py:131
  255.3 1.5 bitcast_dynamic-update-slice_fusion.2
  256.8 1.5 bitcast_dynamic-update-slice_fusion.2
  258.2 1.5 bitcast_dynamic-update-slice_fusion.2
  259.7 1.5 bitcast_dynamic-update-slice_fusion.2
  261.2 1.5 bitcast_dynamic-update-slice_fusion.2
  262.7 1.5 bitcast_dynamic-update-slice_fusion.2
  264.1 1.5 bitcast_dynamic-update-slice_fusion.2
  265.6 1.5 bitcast_dynamic-update-slice_fusion.2
  267.1 1.5 bitcast_dynamic-update-slice_fusion.2
  268.5 1.5 bitcast_dynamic-update-slice_fusion.2
  270.0 1.5 bitcast_dynamic-update-slice_fusion.2
  271.5 1.5 bitcast_dynamic-update-slice_fusion.2
  272.9 1.5 bitcast_dynamic-update-slice_fusion.2
  274.4 1.5 bitcast_dynamic-update-slice_fusion.2
  275.9 1.5 bitcast_dynamic-update-slice_fusion.2
  277.4 1.5 bitcast_dynamic-update-slice_fusion.2
  278.8 1.5 bitcast_dynamic-update-slice_fusion.2
  280.3 1.5 bitcast_dynamic-update-slice_fusion.2
  281.8 1.5 bitcast_dynamic-update-slice_fusion.2
  283.3 1.5 bitcast_dynamic-update-slice_fusion.2
  284.7 1.5 bitcast_dynamic-update-slice_fusion.2
  286.2 1.5 bitcast_dynamic-update-slice_fusion.2
  287.7 1.5 bitcast_dynamic-update-slice_fusion.2
  289.1 1.5 bitcast_dynamic-update-slice_fusion.2
  290.6 1.5 bitcast_dynamic-update-slice_fusion.2
  292.1 1.5 bitcast_dynamic-update-slice_fusion.2
  293.5 1.5 bitcast_dynamic-update-slice_fusion.2
  295.0 1.5 bitcast_dynamic-update-slice_fusion.2
  296.5 1.5 bitcast_dynamic-update-slice_fusion.2
  305.4 3.7 fusion.78
  309.1 3.4 convolution_subtract_fusion
  312.6 16.7 %while.127 = (s32[]{:T(128)}, f32[128,128]{0,1:T(8,128)S(1)}, f32[16,128]{1,0:T(8,128)S(1)}, f32[32,128,128]{2,1,0:T(8,128)S(1)}, f32[32,16,128]{2,1,0:T(8,128)S(1)}, /*index=5*/s32[]{:T(128)}, s32[]{:T(128)}, s32[]{:T(128)}) while((s32[]{:T(128)}, f32[128,128]{0,1:T(8,128)S(1)}, f32[16,128]{1,0:T(8,128)S(1)}, ...), condition=%wide.region_13.14_spmd.clone, body=%wide.region_12.13_spmd.clone.sunk | while | flops 28315652 | bytes 435822 | solution.py:137
  329.2 10.1 %all-gather.4 = f32[512,128]{0,1:T(8,128)S(1)} all-gather(f32[128,128]{0,1:T(8,128)S(1)} %get-tuple-element.764), channel_id=6, replica_groups=mesh['track'=4,'tm'=8] {'track'}, dimensions={0}, use_global_device_ids=true | all-gather | bytes 327680 | tf_op jit(solution)/shard_map/all_gather | solution.py:10
  339.4 7.5 %all-gather.5 = f32[64,128]{1,0:T(8,128)S(1)} all-gather(f32[16,128]{1,0:T(8,128)S(1)} %get-tuple-element.765), channel_id=7, replica_groups=mesh['track'=4,'tm'=8] {'track'}, dimensions={0}, use_global_device_ids=true | all-gather | bytes 40960 | tf_op jit(solution)/shard_map/all_gather | solution.py:10
  346.9 2.1 while.128
  349.6 8.8 %all_gather.69 = f32[4,144,128]{2,1,0:T(8,128)S(1)} all-gather(f32[1,144,128]{2,1,0:T(8,128)S(1)} %maximum_select_fusion.1), channel_id=1, replica_groups=mesh['track'=4,'tm'=8] {'track'}, dimensions={0}, use_global_device_ids=true | all-gather | bytes 368640 | tf_op jit(solution)/shard_map/all_gather | solution.py:28
  358.5 14.9 %all-gather.6 = f32[1024,128]{1,0:T(8,128)S(1)} all-gather(f32[128,128]{1,0:T(8,128)S(1)} %slice.61), channel_id=8, replica_groups=mesh['track'=4,'tm'=8] {'tm'}, dimensions={0}, use_global_device_ids=true | all-gather | bytes 589824 | tf_op jit(solution)/shard_map/all_gather | solution.py:10
  373.4 13.9 %all-gather.7 = f32[128,128]{1,0:T(8,128)S(1)} all-gather(f32[16,128]{1,0:T(8,128)S(1)} %slice.62), channel_id=9, replica_groups=mesh['track'=4,'tm'=8] {'tm'}, dimensions={0}, use_global_device_ids=true | all-gather | bytes 73728 | tf_op jit(solution)/shard_map/all_gather | solution.py:10
  387.3 1.5 while.129
  389.1 8.2 %while.123 = (s32[]{:T(128)}, f32[16,128]{1,0:T(8,128)S(1)}, f32[32,16,128]{2,0,1:T(8,128)S(1)}, f32[32,16,128]{2,1,0:T(8,128)S(1)}, f32[32,128,128]{2,1,0:T(8,128)S(1)}, /*index=5*/s32[]{:T(128)}, s32[]{:T(128)}, s32[]{:T(128)}) while((s32[]{:T(128)}, f32[16,128]{1,0:T(8,128)S(1)}, f32[32,16,128]{2,0,1:T(8,128)S(1)}, ...), condition=%wide.region_20.21_spmd, body=%wide.region_19.20_spmd.sunk | while | flops 3147779 | bytes 124005 | solution.py:141
  397.3 8.9 %all_to_all.36 = f32[32,16,128]{2,0,1:T(8,128)S(1)} all-to-all(f32[32,16,128]{2,0,1:T(8,128)S(1)} %get-tuple-element.769), channel_id=1, replica_groups=mesh['track'=4,'tm'=8] {'track'}, dimensions={1} | all-to-all | bytes 524288 | tf_op jit(solution)/shard_map/all_to_all | solution.py:172
  (529 shorter events, 121.8 us)
Async XLA Ops:
  6.5 19.4 %copy-start = (bf16[64,128]{1,0:T(8,128)(2,1)S(1)}, bf16[64,128]{1,0:T(8,128)(2,1)}, u32[]{:S(2)}) copy-start(bf16[64,128]{1,0:T(8,128)(2,1)} %param.26) | copy-start | bytes 49156
  6.5 9.7 %copy-start.6 = (bf16[64,128,128]{2,1,0:T(8,128)(2,1)S(1)}, bf16[64,128,128]{2,1,0:T(8,128)(2,1)}, u32[]{:S(2)}) copy-start(bf16[64,128,128]{2,1,0:T(8,128)(2,1)} %param.25) | copy-start | bytes 6291460
  6.5 95.0 %all-reduce.6.cloned.1.call-start = ((), (), s32[]{:S(2)}) async-start(), calls=%async_computation.2 | async-start | bytes 5242880
  6.5 3.3 collective-permute-start
  18.9 5.3 %copy-start.15 = (u32[32]{0:T(128)S(1)}, u32[32]{0:T(128)}, u32[]{:S(2)}) copy-start(u32[32]{0:T(128)} %constant.255) | copy-start | bytes 388
  18.9 25.4 %all-to-all-start = ((f32[128,4,128]{2,1,0:T(4,128)}), f32[128,4,128]{2,1,0:T(4,128)S(1)}, u32[]{:S(2)}, u32[]{:S(2)}) async-start(f32[128,4,128]{2,1,0:T(4,128)} %param.23), calls=%async_computation | async-start | bytes 524288 | tf_op jit(solution)/shard_map/all_to_all | solution.py:169
  24.1 80.0 %copy-start.1 = (f32[128,128]{0,1:T(8,128)}, f32[128,128]{0,1:T(8,128)S(1)}, u32[]{:S(2)}) copy-start(f32[128,128]{0,1:T(8,128)S(1)} %fusion.84) | copy-start | bytes 196612
  101.5 3.7 copy-start.13
  104.2 2.4 copy-start.3
  106.5 78.3 %copy-start.4 = (f32[128,128]{0,1:T(8,128)S(1)}, f32[128,128]{0,1:T(8,128)}, u32[]{:S(2)}) copy-start(f32[128,128]{0,1:T(8,128)} %copy-done.1) | copy-start | bytes 196612
  163.8 0.7 copy-start.7
  194.7 59.7 %copy-start.10 = (f32[16,128]{1,0:T(8,128)S(1)}, f32[16,128]{1,0:T(8,128)}, u32[]{:S(2)}) copy-start(f32[16,128]{1,0:T(8,128)} %get-tuple-element.761) | copy-start | bytes 24580
  304.3 0.7 copy-start.14
  305.4 3.7 copy-start.12
  309.1 3.4 copy-start.5
  309.1 3.4 copy-start.8
  312.5 34.4 %copy-start.2 = (f32[128,128]{0,1:T(8,128)S(1)}, f32[128,128]{0,1:T(8,128)}, u32[]{:S(2)}) copy-start(f32[128,128]{0,1:T(8,128)} %copy-done.1) | copy-start | bytes 196612
  312.5 34.4 %copy-start.9 = (f32[16,128]{1,0:T(8,128)S(1)}, f32[16,128]{1,0:T(8,128)}, u32[]{:S(2)}) copy-start(f32[16,128]{1,0:T(8,128)} %custom-call.4) | copy-start | bytes 24580
  346.9 40.4 %copy-start.11 = (f32[16,128]{1,0:T(8,128)S(1)}, f32[16,128]{1,0:T(8,128)}, u32[]{:S(2)}) copy-start(f32[16,128]{1,0:T(8,128)} %custom-call.5) | copy-start | bytes 24580
Sparse Core Ops, SparseCore 0:
  19.0 82.4 all-reduce.5
